TPU v7x, 32 devices: a whole 2x2x4 slice. The times are simulated.
32 devices in a mesh: mode: 2 (over y), col: 16 (over z, x, core).
Axes of the slice: x: 2, y: 2, z: 4, core: 2. Of those that a mesh axis runs over, the one named last changes fastest.
Arguments:
- tensor: float32 [512, 16, 4096], P('mode', 'col'), may hold values from -15 to 15
- start_basis: float32 [512, 128], replicated, may hold values from -6 to 6
Outputs:
- factor: float32 [512, 512], replicated
- basis: float32 [512, 128], replicated
- core: float32 [128, 16, 4096], P(None, 'col', 'mode')
All inputs are finite; a program needn't handle non-finite values.
Results may differ from a plain program's by a relative error of at most 0.00018.
Values sent between devices are 32-bit elements; how exact they have to be, the bound alone decides.
A program may use at most 64 MiB of HBM per device.

v0:
```python
import jax
import jax.numpy as jnp
from jax import lax
from jax.sharding import PartitionSpec as P

POWER = 2


def matmul(left, right):
    return jnp.dot(left, right, precision=lax.Precision.HIGHEST, preferred_element_type=jnp.float32)


def orthonormal(image):
    small = jnp.linalg.cholesky(matmul(image.T, image))
    return jax.scipy.linalg.solve_triangular(small, image.T, lower=True).T


def per_device(tensor, start_basis):
    regrouped = lax.all_to_all(tensor, "mode", split_axis=2, concat_axis=0, tiled=True)
    rows = regrouped.shape[0]
    flat = regrouped.reshape(rows, -1)
    columns = flat.shape[1] * lax.axis_size("mode") * lax.axis_size("col")
    gram = matmul(flat, flat.T)
    total = lax.psum(gram, ("mode", "col"))
    factor = jnp.linalg.cholesky(total / columns)
    basis = start_basis
    for step in range(POWER):
        image = matmul(factor, matmul(factor.T, basis))
        basis = orthonormal(image)
    core = matmul(basis.T, flat).reshape(basis.shape[1], regrouped.shape[1], regrouped.shape[2])
    return (factor, basis, core)


def solution(mesh):
    in_specs = (P("mode", "col", None), P())
    out_specs = (P(), P(), P(None, "col", "mode"))
    return jax.shard_map(
        per_device, mesh=mesh, in_specs=in_specs, out_specs=out_specs, check_vma=False
    )
```

profile of v0, /device:TPU:0, one launch (start us, length us, event | category | flops | bytes accessed | tf_op | source)
XLA Modules:
  0.0 378.2 jit_solution(11997995047091231864)
XLA Ops:
  7.2 0.0 copy-start
  7.2 0.0 all-reduce.3.cloned.1.call-start
  7.2 14.3 %copy.25 = f32[256,1,4096]{0,1,2:T(1,128)} copy(f32[256,1,4096]{2,1,0:T(1,128)} %param.5) | data formatting | bytes 8388608 | tf_op args[0]
  21.5 52.9 %all_to_all.15 = f32[256,1,4096]{0,1,2:T(1,128)S(1)} all-to-all(f32[256,1,4096]{0,1,2:T(1,128)} %copy.25), channel_id=1, replica_groups=mesh['mode'=2,'col'=16] {'mode'}, dimensions={2} | all-to-all | bytes 8388608 | tf_op jit(solution)/shard_map/all_to_all | solution.py:19
  74.4 2.2 copy.34
  76.7 5.4 %copy.26 = f32[2,256,1,2048]{3,1,0,2:T(8,128)} copy(f32[2,256,1,2048]{1,3,0,2:T(8,128)} %bitcast.71) | data formatting | bytes 8388608 | tf_op jit(solution)/shard_map/all_to_all | solution.py:19
  82.1 10.6 %fusion.22 = f32[512,512]{0,1:T(8,128)} fusion(f32[512,2048]{1,0:T(8,128)} %bitcast.69), kind=kOutput, calls=%fused_computation.57 | convolution fusion | flops 6442450944 | bytes 5242880 | tf_op jit(solution)/shard_map/dot_general | solution.py:10
  92.7 0.0 all-reduce.3.cloned.1.call-update
  92.7 131.3 %all-reduce.3.cloned.1.call-done = f32[512,512]{0,1:T(8,128)} async-done(((f32[512,512]{0,1:T(8,128)}), f32[512,512]{0,1:T(8,128)}) %all-reduce.3.cloned.1.call-update) | async-done | bytes 1048592 | tf_op jit(solution)/shard_map/psum | solution.py:24
  224.0 0.0 copy-start.2
  224.0 1.4 broadcast_multiply_fusion
  225.5 0.3 copy.28
  225.8 0.0 copy-done.2
  225.8 0.2 fusion
  226.1 11.7 %cholesky.120 = f32[128,128]{1,0:T(8,128)S(1)} custom-call(f32[128,128]{1,0:T(8,128)S(1)} %cholesky.330), custom_call_target="Cholesky" | custom-call | tf_op jit(solution)/shard_map/jit(cholesky)/cholesky | solution.py:25
  237.8 9.8 %custom-call.32 = f32[1,128,128]{1,2,0:T(8,128)S(1)} custom-call(f32[1,128,128]{2,1,0:T(8,128)S(1)} %get-tuple-element.26), custom_call_target="InvertDiagBlocksLowerTriangular" | custom-call | tf_op jit(solution)/shard_map/jit(cholesky)/cholesky | solution.py:25
  247.6 0.1 cholesky.251
  247.8 0.3 constant_dynamic-update-slice_fusion.2
  248.1 0.3 convolution_subtract_fusion
  248.4 11.7 %cholesky.244 = f32[128,128]{1,0:T(8,128)S(1)} custom-call(f32[128,128]{1,0:T(8,128)S(1)} %cholesky.334), custom_call_target="Cholesky" | custom-call | tf_op jit(solution)/shard_map/jit(cholesky)/cholesky | solution.py:25
  260.2 9.9 %custom-call.33 = f32[1,128,128]{1,2,0:T(8,128)S(1)} custom-call(f32[1,128,128]{2,1,0:T(8,128)S(1)} %get-tuple-element.23), custom_call_target="InvertDiagBlocksLowerTriangular" | custom-call | tf_op jit(solution)/shard_map/jit(cholesky)/cholesky | solution.py:25
  270.1 0.3 convolution_dynamic-update-slice_fusion
  270.4 0.4 convolution_subtract_fusion.1
  270.8 11.7 %cholesky.265 = f32[128,128]{1,0:T(8,128)S(1)} custom-call(f32[128,128]{1,0:T(8,128)S(1)} %cholesky.339), custom_call_target="Cholesky" | custom-call | tf_op jit(solution)/shard_map/jit(cholesky)/cholesky | solution.py:25
  282.5 0.6 compare_reduce_fusion.3
  283.2 9.8 %custom-call.34 = f32[1,128,128]{1,2,0:T(8,128)S(1)} custom-call(f32[1,128,128]{2,1,0:T(8,128)S(1)} %get-tuple-element.20), custom_call_target="InvertDiagBlocksLowerTriangular" | custom-call | tf_op jit(solution)/shard_map/jit(cholesky)/cholesky | solution.py:25
  293.0 0.2 convolution_dynamic-update-slice_fusion.1
  293.2 0.4 convolution_subtract_fusion.2
  293.6 11.7 %cholesky.282 = f32[128,128]{1,0:T(8,128)S(1)} custom-call(f32[128,128]{1,0:T(8,128)S(1)} %convolution_subtract_fusion.2), custom_call_target="Cholesky" | custom-call | tf_op jit(solution)/shard_map/jit(cholesky)/cholesky | solution.py:25
  305.3 0.7 compare_reduce_fusion.2
  306.0 0.6 compare_reduce_fusion.4
  309.4 0.1 select_select_fusion
  309.5 0.0 copy-done
  309.5 0.0 copy-start.1
  309.5 1.8 fusion.23
  311.4 1.0 fusion.24
  312.4 0.6 fusion.25
  312.9 0.1 copy.29
  313.1 11.7 %cholesky.310 = f32[128,128]{1,0:T(8,128)S(1)} custom-call(f32[128,128]{1,0:T(8,128)S(1)} %fusion.18), custom_call_target="Cholesky" | custom-call | tf_op jit(solution)/shard_map/jit(cholesky)/cholesky | solution.py:14
  324.8 0.6 compare_reduce_fusion.1
  325.5 0.7 fusion.11
  326.1 9.8 %custom-call.36 = f32[1,128,128]{1,2,0:T(8,128)S(1)} custom-call(f32[1,128,128]{2,1,0:T(8,128)S(1)} %fusion.11), custom_call_target="InvertDiagBlocksLowerTriangular" | custom-call | tf_op jit(solution)/shard_map/jit(_solve_triangular)/triangular_solve | solution.py:15
  335.9 0.4 fusion.4
  336.4 1.8 fusion.26
  338.2 1.3 fusion.27
  339.4 0.6 fusion.28
  340.0 0.0 copy-done.1
  340.0 0.1 copy.30
  340.1 11.7 %cholesky.321 = f32[128,128]{1,0:T(8,128)S(1)} custom-call(f32[128,128]{1,0:T(8,128)S(1)} %fusion.16), custom_call_target="Cholesky" | custom-call | tf_op jit(solution)/shard_map/jit(cholesky)/cholesky | solution.py:14
  351.9 0.6 compare_reduce_fusion
  352.5 0.7 fusion.12
  353.2 9.8 %custom-call.37 = f32[1,128,128]{1,2,0:T(8,128)S(1)} custom-call(f32[1,128,128]{2,1,0:T(8,128)S(1)} %fusion.12), custom_call_target="InvertDiagBlocksLowerTriangular" | custom-call | tf_op jit(solution)/shard_map/jit(_solve_triangular)/triangular_solve | solution.py:15
  363.0 0.4 fusion.2
  363.4 4.6 %convolution_bitcast_fusion = f32[128,1,2048]{2,0,1:T(8,128)S(1)} fusion(f32[128,512]{1,0:T(8,128)S(1)} %fusion.2, f32[512,2048]{1,0:T(8,128)} %bitcast.70), kind=kOutput, calls=%fused_computation | convolution fusion | flops 1610612736 | bytes 5505024 | tf_op jit(solution)/shard_map/dot_general | solution.py:10
  368.0 2.0 copy.32
  370.0 0.8 copy.31
  (11 shorter events, 0.3 us)
Async XLA Ops:
  7.2 302.4 %copy-start = (f32[512,128]{1,0:T(8,128)S(1)}, f32[512,128]{1,0:T(8,128)}, u32[]{:S(2)}) copy-start(f32[512,128]{1,0:T(8,128)} %param.6) | copy-start | bytes 786436
  7.2 216.9 %all-reduce.3.cloned.1.call-start = ((), (), s32[]{:S(2)}) async-start(), calls=%async_computation.1 | async-start | bytes 2097152 | tf_op jit(solution)/shard_map/psum | solution.py:24
  224.0 1.8 copy-start.2
  309.5 30.5 %copy-start.1 = (f32[512,512]{1,0:T(8,128)}, f32[512,512]{1,0:T(8,128)S(1)}, u32[]{:S(2)}) copy-start(f32[512,512]{1,0:T(8,128)S(1)} %select_select_fusion) | copy-start | bytes 3145732
Sparse Core Ops, SparseCore 0:
  92.9 131.1 all-reduce.2
where the time goes:
time: 383 us; the launch traced here: 378 us
  waiting for transfers between devices  131 us (34%)
  other arithmetic  126 us (33%)
  blocking collectives  52.9 us (14%)
  local copies, waits for them, and re-layouts  25.4 us (7%)
  matrix products  24.9 us (7%)
  between operations  17.5 us (5%)
    psum x1, waiting for transfers between devices, per_device(): total = lax.psum(gram, ('mode', 'col'))  131 us
    another operation x14, other arithmetic, per_device(): factor = jnp.linalg.cholesky(total / columns)  78.5 us
    all_to_all x1, blocking collectives, per_device(): lax.all_to_all(tensor, 'mode', split_axis=2, concat_axis=0, tiled=True)  52.9 us
    another operation x6, other arithmetic, orthonormal(): small = jnp.linalg.cholesky(matmul(image.T, image))  24.8 us
    dot_general x8, matrix products, matmul(): jnp.dot(left, right, precision=lax.Precision.HIGHEST, preferred_element_t...  22.2 us
    another operation x4, other arithmetic, orthonormal(): return jax.scipy.linalg.solve_triangular(small, image.T, lower=True).T  20.9 us
    unnamed x10, local copies, waits for them, and re-layouts  19.4 us
  transfers between devices with their start and end apart: 1, of which 1 were waited for; matrix products, arithmetic and copies ran while one was open for 0% of the time, Pallas kernels for 0%

commit v1 on v0

v1 whole, which is shorter than its diff:
```python
import functools

import jax
import jax.numpy as jnp
from jax import lax
from jax.experimental import pallas as pl
from jax.experimental.pallas import tpu as pltpu
from jax.sharding import PartitionSpec as P

POWER = 2
BLOCK = 128
PANEL = 8


def halves(value):
    high = value.astype(jnp.bfloat16)
    low = (value - high.astype(jnp.float32)).astype(jnp.bfloat16)
    return high, low


def contract(left, right, dims):
    return lax.dot_general(left, right, (dims, ((), ())), preferred_element_type=jnp.float32)


def exact(left, right, dims):
    return lax.dot_general(
        left, right, (dims, ((), ())), precision=lax.Precision.HIGHEST,
        preferred_element_type=jnp.float32,
    )


NN = ((1,), (0,))
NT = ((1,), (1,))
TN = ((0,), (0,))


def split3(value):
    high = value.astype(jnp.bfloat16).astype(jnp.float32)
    rest = value - high
    middle = rest.astype(jnp.bfloat16).astype(jnp.float32)
    return high, middle, rest - middle


def eliminate_panel(aug, j):
    size, width = aug.shape
    first = PANEL * j
    rows = [aug[first + t : first + t + 1, :] for t in range(PANEL)]
    entry = {}
    for t in range(PANEL):
        for s in range(t, PANEL):
            value = rows[t][:, first + s : first + s + 1]
            entry[s, t] = jnp.broadcast_to(value, (1, size))
    pivots = []
    for t in range(PANEL):
        pivot = entry[t, t]
        pivots.append(pivot)
        inverse = 1.0 / pivot
        for s in range(t + 1, PANEL):
            ratio = entry[s, t] * inverse
            for u in range(s, PANEL):
                entry[u, s] = entry[u, s] - ratio * entry[u, t]
            rows[s] = rows[s] - jnp.concatenate([ratio] * (width // size), axis=1) * rows[t]
    done = []
    for t in range(PANEL):
        scale = lax.rsqrt(pivots[t])
        done.append(rows[t] * jnp.concatenate([scale] * (width // size), axis=1))
    panel = jnp.concatenate(done, axis=0)
    aug[first : first + PANEL, :] = panel
    below = first + PANEL
    if below < size:
        high, middle, low = split3(panel)
        left = jnp.concatenate([high, high, middle, high, low, middle], axis=0).astype(jnp.bfloat16)
        right = jnp.concatenate([high, middle, high, low, high, middle], axis=0).astype(jnp.bfloat16)
        aug[below:size, :] = aug[below:size, :] - contract(left[:, below:size], right, TN)


def eliminate(augs):
    for j in range(BLOCK // PANEL):
        for aug in augs:
            eliminate_panel(aug, j)


def load_augmented(aug, matrix):
    size = matrix.shape[0]
    row = lax.broadcasted_iota(jnp.int32, (size, size), 0)
    column = lax.broadcasted_iota(jnp.int32, (size, size), 1)
    aug[:, 0:size] = matrix
    aug[:, size : 2 * size] = jnp.where(row == column, 1.0, 0.0).astype(jnp.float32)


def linear_kernel(columns, gram_ref, start_ref, flat_ref, factor_ref, basis_ref, core_ref, gram, work, image, aug_f, aug_b):
    size, rank = start_ref.shape
    blocks = size // BLOCK
    row = lax.broadcasted_iota(jnp.int32, (BLOCK, BLOCK), 0)
    column = lax.broadcasted_iota(jnp.int32, (BLOCK, BLOCK), 1)
    scale = 1.0 / columns
    scaled = gram_ref[...] * scale
    gram[...] = scaled
    work[...] = scaled

    for step in range(max(blocks, POWER)):
        augs = []
        if step < blocks:
            at = step * BLOCK
            load_augmented(aug_f, work[at : at + BLOCK, at : at + BLOCK])
            augs.append(aug_f)
        if step < POWER:
            source = start_ref if step == 0 else basis_ref
            image[...] = exact(gram[...], source[...], NN)
            load_augmented(aug_b, exact(image[...], image[...], TN))
            augs.append(aug_b)
        eliminate(augs)
        if step < POWER:
            basis_ref[...] = exact(image[...], aug_b[:, rank : 2 * rank], NT)
        if step < blocks:
            upper = jnp.where(row <= column, aug_f[:, 0:BLOCK], 0.0)
            factor_ref[at : at + BLOCK, at : at + BLOCK] = upper.T
            if step > 0:
                factor_ref[0:at, at : at + BLOCK] = jnp.zeros((at, BLOCK), jnp.float32)
            below = at + BLOCK
            if below < size:
                inverse = aug_f[:, BLOCK : 2 * BLOCK]
                left = exact(work[below:size, at : at + BLOCK], inverse, NT)
                factor_ref[below:size, at : at + BLOCK] = left
                work[below:size, below:size] = work[below:size, below:size] - exact(left, left, NT)

    high, low = halves(basis_ref[...])
    width = 512
    for start in range(0, flat_ref.shape[1], width):
        flat_high, flat_low = halves(flat_ref[:, start : start + width])
        core_ref[:, start : start + width] = (
            contract(high, flat_high, TN) + contract(high, flat_low, TN) + contract(low, flat_high, TN)
        )


def linear(columns, gram, start_basis, flat):
    size, rank = start_basis.shape
    vmem = pl.BlockSpec(memory_space=pltpu.VMEM)
    return pl.pallas_call(
        functools.partial(linear_kernel, columns),
        out_shape=(
            jax.ShapeDtypeStruct((size, size), jnp.float32),
            jax.ShapeDtypeStruct((size, rank), jnp.float32),
            jax.ShapeDtypeStruct((rank, flat.shape[1]), jnp.float32),
        ),
        in_specs=[vmem] * 3,
        out_specs=(vmem,) * 3,
        scratch_shapes=[
            pltpu.VMEM((size, size), jnp.float32),
            pltpu.VMEM((size, size), jnp.float32),
            pltpu.VMEM((size, rank), jnp.float32),
            pltpu.VMEM((BLOCK, 2 * BLOCK), jnp.float32),
            pltpu.VMEM((rank, 2 * rank), jnp.float32),
        ],
        name="linear",
    )(gram, start_basis, flat)


def matmul(left, right):
    return jnp.dot(left, right, precision=lax.Precision.HIGHEST, preferred_element_type=jnp.float32)


def per_device(tensor, start_basis):
    regrouped = lax.all_to_all(tensor, "mode", split_axis=2, concat_axis=0, tiled=True)
    rows = regrouped.shape[0]
    flat = regrouped.reshape(rows, -1)
    columns = flat.shape[1] * lax.axis_size("mode") * lax.axis_size("col")
    gram = matmul(flat, flat.T)
    total = lax.psum(gram, ("mode", "col"))
    factor, basis, core = linear(columns, total, start_basis, flat)
    return (factor, basis, core.reshape(basis.shape[1], regrouped.shape[1], regrouped.shape[2]))


def solution(mesh):
    in_specs = (P("mode", "col", None), P())
    out_specs = (P(), P(), P(None, "col", "mode"))
    return jax.shard_map(
        per_device, mesh=mesh, in_specs=in_specs, out_specs=out_specs, check_vma=False
    )
```

time: 383 us -> 272 us (0.71); the launches traced: 378 us -> 271 us
  other arithmetic: 126 us -> 0 us
  Pallas kernels: 0 us -> 37.4 us
  matrix products: 24.9 us -> 10.3 us
    another operation x24 -> x0, other arithmetic: 124 us -> none  [the longest x14 78.5 us: per_device(): factor = jnp.linalg.cholesky(total / columns)]
    pallas_call x0 -> x1, Pallas kernels: none -> 37.4 us  [linear(): pl.pallas_call(functools.partial(linear_kernel, columns), out_shape=(jax....]
    dot_general x8 -> x1, matrix products: 22.2 us -> 10.3 us  [matmul(): jnp.dot(left, right, precision=lax.Precision.HIGHEST, preferred_element_t...]
    unnamed x10 -> x3, local copies, waits for them, and re-layouts: 19.4 us -> 19.7 us
where the time goes in v1:
time: 272 us; the launch traced here: 271 us
  waiting for transfers between devices  131 us (48%)
  blocking collectives  52.9 us (19%)
  Pallas kernels  37.4 us (14%)
  local copies, waits for them, and re-layouts  25.2 us (9%)
  between operations  14 us (5%)
  matrix products  10.3 us (4%)
    psum x1, waiting for transfers between devices, per_device(): total = lax.psum(gram, ('mode', 'col'))  131 us
    all_to_all x1, blocking collectives, per_device(): lax.all_to_all(tensor, 'mode', split_axis=2, concat_axis=0, tiled=True)  52.9 us
    pallas_call x1, Pallas kernels, linear(): pl.pallas_call(functools.partial(linear_kernel, columns), out_shape=(jax....  37.4 us
    unnamed x3, local copies, waits for them, and re-layouts  19.7 us
    dot_general x1, matrix products, matmul(): jnp.dot(left, right, precision=lax.Precision.HIGHEST, preferred_element_t...  10.3 us
    all_to_all x1, local copies, waits for them, and re-layouts, per_device(): lax.all_to_all(tensor, 'mode', split_axis=2, concat_axis=0, tiled=True)  5.46 us
  transfers between devices with their start and end apart: 1, of which 1 were waited for; matrix products, arithmetic and copies ran while one was open for 0% of the time, Pallas kernels for 0%

profile of v1, /device:TPU:0, one launch (start us, length us, event | category | flops | bytes accessed | tf_op | source)
XLA Modules:
  0.0 271.3 jit_solution(16030631476568042222)
XLA Ops:
  7.2 0.0 all-reduce.2.cloned.1.call-start
  7.2 14.2 %copy.13 = f32[256,1,4096]{0,1,2:T(1,128)} copy(f32[256,1,4096]{2,1,0:T(1,128)} %param.2) | data formatting | bytes 8388608 | tf_op args[0]
  21.5 52.9 %all_to_all.15 = f32[256,1,4096]{0,1,2:T(1,128)S(1)} all-to-all(f32[256,1,4096]{0,1,2:T(1,128)} %copy.13), channel_id=1, replica_groups=mesh['mode'=2,'col'=16] {'mode'}, dimensions={2} | all-to-all | bytes 8388608 | tf_op jit(solution)/shard_map/all_to_all | solution.py:164
  74.4 2.2 copy.16
  76.6 5.5 %copy.14 = f32[2,256,1,2048]{3,1,0,2:T(8,128)} copy(f32[2,256,1,2048]{1,3,0,2:T(8,128)} %bitcast.9) | data formatting | bytes 8388608 | tf_op jit(solution)/shard_map/all_to_all | solution.py:164
  82.1 10.3 %fusion = f32[512,512]{1,0:T(8,128)} fusion(f32[512,2048]{1,0:T(8,128)} %bitcast.7), kind=kOutput, calls=%fused_computation | convolution fusion | flops 6442450944 | bytes 5242880 | tf_op jit(solution)/shard_map/dot_general | solution.py:160
  92.3 0.0 all-reduce.2.cloned.1.call-update
  92.4 131.3 %all-reduce.2.cloned.1.call-done.gram_ref = f32[512,512]{1,0:T(8,128)} async-done(((f32[512,512]{1,0:T(8,128)}), f32[512,512]{1,0:T(8,128)}) %all-reduce.2.cloned.1.call-update) | async-done | bytes 1048592 | tf_op jit(solution)/shard_map/psum | solution.py:169
  223.7 37.4 %linear.1 = (f32[512,512]{1,0:T(8,128)}, f32[512,128]{1,0:T(8,128)}, f32[128,2048]{1,0:T(8,128)}) custom-call(f32[512,512]{1,0:T(8,128)} %all-reduce.2.cloned.1.call-done.gram_ref, f32[512,128]{1,0:T(8,128)} %start_ref.1, f32[512,2048]{1,0:T(8,128)} %bitcast.8), custom_call_target="tpu_custom_call" | custom-call | tf_op jit(solution)/shard_map/linear/pallas_call | solution.py:139
  261.1 3.3 %copy.15 = f32[128,1,2048]{2,1,0:T(1,128)} copy(f32[128,1,2048]{2,0,1:T(8,128)} %bitcast.10) | data formatting | bytes 2097152
Async XLA Ops:
  7.2 216.5 %all-reduce.2.cloned.1.call-start = ((), (), s32[]{:S(2)}) async-start(), calls=%async_computation.1 | async-start | bytes 2097152 | tf_op jit(solution)/shard_map/psum | solution.py:169
Sparse Core Ops, SparseCore 0:
  92.5 131.1 all-reduce.1

commit v2 on v1

--- a/solution.py
+++ b/solution.py
@@ -10,6 +10,8 @@
 POWER = 2
 BLOCK = 128
 PANEL = 8
+CHUNK = 512
+MESH = pl.DeviceIdType.MESH
 
 
 def halves(value):
@@ -88,15 +90,227 @@
     aug[:, size : 2 * size] = jnp.where(row == column, 1.0, 0.0).astype(jnp.float32)
 
 
-def linear_kernel(columns, gram_ref, start_ref, flat_ref, factor_ref, basis_ref, core_ref, gram, work, image, aug_f, aug_b):
+def lower_blocks(blocks):
+    return [(i, k) for i in range(blocks) for k in range(i + 1)]
+
+
+def stages_of(modes, cols):
+    stages, stride = [], 1
+    first = 2 if cols % 2 == 0 else 1
+    if first > 1:
+        stages.append((1, first, False))
+        stride = first
+    second = 2 if (cols // stride) % 2 == 0 else 1
+    stages.append((stride, second, True))
+    stride *= second
+    if cols // stride > 1:
+        stages.append((stride, cols // stride, False))
+    return stages
+
+
+def gather_kernel(modes, cols, x_ref, flat_ref, total_ref, acc, main, cross, *rest):
+    mode, col = lax.axis_index("mode"), lax.axis_index("col")
+    stages = stages_of(modes, cols)
+    slots = rest[: len(stages)]
+    own_sem, piece_send, piece_recv, sum_send, sum_recv, share_send, share_recv = rest[len(stages) :]
+    rows, depth, length = x_ref.shape
+    size = rows * modes
+    width = length // modes
+    chunk = min(CHUNK, width)
+    per = width // chunk
+    chunks = depth * per
+
+    def position(stage):
+        stride, count, with_mode = stage
+        place = lax.rem(lax.div(col, stride), count)
+        return place * modes + mode if with_mode else place
+
+    def members(stage):
+        return stage[1] * (modes if stage[2] else 1)
+
+    def peer(stage, offset):
+        stride, count, with_mode = stage
+        other = lax.rem(position(stage) + offset, members(stage))
+        place = lax.div(other, modes) if with_mode else other
+        there = col + (place - lax.rem(lax.div(col, stride), count)) * stride
+        return other, (lax.rem(other, modes) if with_mode else mode, there)
+
+    partners = [(lax.rem(mode + d, modes), col) for d in range(1, modes)]
+    greeted = [] if any(stage[2] for stage in stages) else list(partners)
+    for stage in stages:
+        greeted += [peer(stage, d)[1] for d in range(1, members(stage))]
+    barrier = pltpu.get_barrier_semaphore()
+    for device in greeted:
+        pl.semaphore_signal(barrier, inc=1, device_id=device, device_id_type=MESH)
+    pl.semaphore_wait(barrier, len(greeted))
+
+    def spans(c):
+        layer, part = lax.div(c, per), lax.rem(c, per)
+        return layer, part * chunk, pl.multiple_of(layer * width + part * chunk, chunk)
+
+    def piece(c, d):
+        layer, start, target = spans(c)
+        source = pl.multiple_of(lax.rem(mode + d, modes) * width + start, chunk)
+        place = pl.ds(pl.multiple_of(mode * rows, rows), rows)
+        return pltpu.make_async_remote_copy(
+            src_ref=x_ref.at[:, layer, pl.ds(source, chunk)],
+            dst_ref=flat_ref.at[place, pl.ds(target, chunk)],
+            send_sem=piece_send.at[d - 1, c],
+            recv_sem=piece_recv.at[d - 1, c],
+            device_id=partners[d - 1],
+            device_id_type=MESH,
+        )
+
+    def own(c):
+        layer, start, target = spans(c)
+        source = pl.multiple_of(mode * width + start, chunk)
+        place = pl.ds(pl.multiple_of(mode * rows, rows), rows)
+        return pltpu.make_async_copy(
+            x_ref.at[:, layer, pl.ds(source, chunk)], flat_ref.at[place, pl.ds(target, chunk)], own_sem.at[c]
+        )
+
+    def begin(c, carry):
+        for d in range(1, modes):
+            piece(c, d).start()
+        own(c).start()
+        return carry
+
+    lax.fori_loop(0, chunks, begin, 0)
+    main[...] = jnp.zeros_like(main)
+    cross[...] = jnp.zeros_like(cross)
+
+    def accumulate(c, carry):
+        own(c).wait()
+        for d in range(1, modes):
+            piece(c, d).wait_recv()
+        target = spans(c)[2]
+        high, low = halves(flat_ref[:, pl.ds(target, chunk)])
+        main[...] += contract(high, high, NT)
+        cross[...] += contract(high, low, NT)
+        return carry
+
+    lax.fori_loop(0, chunks, accumulate, 0)
+
+    blocks = size // BLOCK
+    pairs = lower_blocks(blocks)
+    for n, (i, k) in enumerate(pairs):
+        tall, wide = slice(i * BLOCK, (i + 1) * BLOCK), slice(k * BLOCK, (k + 1) * BLOCK)
+        acc[n * BLOCK : (n + 1) * BLOCK, :] = main[tall, wide] + (cross[tall, wide] + cross[wide, tall].T)
+    used = len(pairs) * BLOCK
+    if used < acc.shape[0]:
+        acc[used:, :] = jnp.zeros((acc.shape[0] - used, BLOCK), jnp.float32)
+
+    base, extent = 0, acc.shape[0]
+    bases = []
+    for g, stage in enumerate(stages):
+        count = members(stage)
+        part = extent // count
+        copies = []
+        for d in range(1, count):
+            other, device = peer(stage, d)
+            copy = pltpu.make_async_remote_copy(
+                src_ref=acc.at[pl.ds(pl.multiple_of(base + other * part, 8), part), :],
+                dst_ref=slots[g].at[d - 1],
+                send_sem=sum_send.at[g, d - 1],
+                recv_sem=sum_recv.at[g, d - 1],
+                device_id=device,
+                device_id_type=MESH,
+            )
+            copy.start()
+            copies.append(copy)
+        base = base + position(stage) * part
+        extent = part
+        bases.append((base, part))
+        for copy in copies:
+            copy.wait()
+        mine = pl.ds(pl.multiple_of(base, 8), part)
+        added = acc[mine, :]
+        for d in range(1, count):
+            added = added + slots[g][d - 1]
+        if g < len(stages) - 1:
+            acc[mine, :] = added
+        else:
+            total_ref[mine, :] = added
+
+    for g in reversed(range(len(stages))):
+        stage = stages[g]
+        base, part = bases[g]
+        mine = pl.ds(pl.multiple_of(base, 8), part)
+        copies = []
+        for d in range(1, members(stage)):
+            copy = pltpu.make_async_remote_copy(
+                src_ref=total_ref.at[mine, :],
+                dst_ref=total_ref.at[mine, :],
+                send_sem=share_send.at[g, d - 1],
+                recv_sem=share_recv.at[g, d - 1],
+                device_id=peer(stage, d)[1],
+                device_id_type=MESH,
+            )
+            copy.start()
+            copies.append(copy)
+        for copy in copies:
+            copy.wait()
+
+    def end(c, carry):
+        for d in range(1, modes):
+            piece(c, d).wait_send()
+        return carry
+
+    lax.fori_loop(0, chunks, end, 0)
+
+
+def gather(tensor):
+    modes, cols = lax.axis_size("mode"), lax.axis_size("col")
+    rows, depth, length = tensor.shape
+    size = rows * modes
+    width = length // modes
+    chunks = depth * (width // min(CHUNK, width))
+    stages = stages_of(modes, cols)
+    unit = 8 * modes * cols
+    packed = -(-(len(lower_blocks(size // BLOCK)) * BLOCK) // unit) * unit
+    slots, extent, most = [], packed, 1
+    for stride, count, with_mode in stages:
+        count = count * (modes if with_mode else 1)
+        extent = extent // count
+        most = max(most, count - 1)
+        slots.append(pltpu.VMEM((max(count - 1, 1), extent, BLOCK), jnp.float32))
+    dma = pltpu.SemaphoreType.DMA
+    vmem = pl.BlockSpec(memory_space=pltpu.VMEM)
+    return pl.pallas_call(
+        functools.partial(gather_kernel, modes, cols),
+        out_shape=(
+            jax.ShapeDtypeStruct((size, depth * width), jnp.float32),
+            jax.ShapeDtypeStruct((packed, BLOCK), jnp.float32),
+        ),
+        in_specs=[pl.BlockSpec(memory_space=pl.ANY)],
+        out_specs=(vmem, vmem),
+        scratch_shapes=[
+            pltpu.VMEM((packed, BLOCK), jnp.float32),
+            pltpu.VMEM((size, size), jnp.float32),
+            pltpu.VMEM((size, size), jnp.float32),
+            *slots,
+            dma((chunks,)),
+            dma((max(modes - 1, 1), chunks)),
+            dma((max(modes - 1, 1), chunks)),
+            *[dma((len(stages), most))] * 4,
+        ],
+        compiler_params=pltpu.CompilerParams(collective_id=0, has_side_effects=True),
+        name="gather",
+    )(tensor)
+
+
+def linear_kernel(columns, packed_ref, start_ref, flat_ref, factor_ref, basis_ref, core_ref, gram, work, image, aug_f, aug_b):
     size, rank = start_ref.shape
     blocks = size // BLOCK
     row = lax.broadcasted_iota(jnp.int32, (BLOCK, BLOCK), 0)
     column = lax.broadcasted_iota(jnp.int32, (BLOCK, BLOCK), 1)
     scale = 1.0 / columns
-    scaled = gram_ref[...] * scale
-    gram[...] = scaled
-    work[...] = scaled
+    for n, (i, k) in enumerate(lower_blocks(blocks)):
+        scaled = packed_ref[n * BLOCK : (n + 1) * BLOCK, :] * scale
+        gram[i * BLOCK : (i + 1) * BLOCK, k * BLOCK : (k + 1) * BLOCK] = scaled
+        work[i * BLOCK : (i + 1) * BLOCK, k * BLOCK : (k + 1) * BLOCK] = scaled
+        if i != k:
+            gram[k * BLOCK : (k + 1) * BLOCK, i * BLOCK : (i + 1) * BLOCK] = scaled.T
 
     for step in range(max(blocks, POWER)):
         augs = []
@@ -133,7 +347,7 @@
         )
 
 
-def linear(columns, gram, start_basis, flat):
+def linear(columns, packed, start_basis, flat):
     size, rank = start_basis.shape
     vmem = pl.BlockSpec(memory_space=pltpu.VMEM)
     return pl.pallas_call(
@@ -153,22 +367,15 @@
             pltpu.VMEM((rank, 2 * rank), jnp.float32),
         ],
         name="linear",
-    )(gram, start_basis, flat)
-
-
-def matmul(left, right):
-    return jnp.dot(left, right, precision=lax.Precision.HIGHEST, preferred_element_type=jnp.float32)
+    )(packed, start_basis, flat)
 
 
 def per_device(tensor, start_basis):
-    regrouped = lax.all_to_all(tensor, "mode", split_axis=2, concat_axis=0, tiled=True)
-    rows = regrouped.shape[0]
-    flat = regrouped.reshape(rows, -1)
+    depth = tensor.shape[1]
+    flat, packed = gather(tensor)
     columns = flat.shape[1] * lax.axis_size("mode") * lax.axis_size("col")
-    gram = matmul(flat, flat.T)
-    total = lax.psum(gram, ("mode", "col"))
-    factor, basis, core = linear(columns, total, start_basis, flat)
-    return (factor, basis, core.reshape(basis.shape[1], regrouped.shape[1], regrouped.shape[2]))
+    factor, basis, core = linear(columns, packed, start_basis, flat)
+    return (factor, basis, core.reshape(basis.shape[1], depth, -1))
 
 
 def solution(mesh):

time: 272 us -> 119 us (0.44)
  waiting for transfers between devices: 131 us -> 0 us
  Pallas kernels: 37.4 us -> 114 us
  blocking collectives: 52.9 us -> 0 us
  local copies, waits for them, and re-layouts: 25.2 us -> 3.27 us
  between operations: 14 us -> 0.64 us
  matrix products: 10.3 us -> 0 us
    psum x1 -> x0, waiting for transfers between devices: 131 us -> none  [per_device(): total = lax.psum(gram, ('mode', 'col'))]
    pallas_call x0 -> x1, Pallas kernels: none -> 77.2 us  [gather(): pl.pallas_call(functools.partial(gather_kernel, modes, cols), out_shape=(...]
    all_to_all x1 -> x0, blocking collectives: 52.9 us -> none  [per_device(): lax.all_to_all(tensor, 'mode', split_axis=2, concat_axis=0, tiled=True)]
    unnamed x3 -> x1, local copies, waits for them, and re-layouts: 19.7 us -> 3.27 us
    dot_general x1 -> x0, matrix products: 10.3 us -> none  [matmul(): jnp.dot(left, right, precision=lax.Precision.HIGHEST, preferred_element_t...]
    all_to_all x1 -> x0, local copies, waits for them, and re-layouts: 5.46 us -> none  [per_device(): lax.all_to_all(tensor, 'mode', split_axis=2, concat_axis=0, tiled=True)]
  transfers between devices with their start and end apart: 1 -> 0, of which waited for: 1 -> 0; matrix products, arithmetic and copies ran while one was open for 0% -> 0% of each run, Pallas kernels for 0% -> 0%
where the time goes in v2:
time: 119 us; the launch traced here: 118 us
  Pallas kernels  114 us (96%)
  local copies, waits for them, and re-layouts  3.27 us (3%)
    pallas_call x1, Pallas kernels, gather(): pl.pallas_call(functools.partial(gather_kernel, modes, cols), out_shape=(...  77.2 us
    pallas_call x1, Pallas kernels, linear(): pl.pallas_call(functools.partial(linear_kernel, columns), out_shape=(jax....  37.3 us
    unnamed x1, local copies, waits for them, and re-layouts  3.27 us

profile of v2, /device:TPU:0, one launch (start us, length us, event | category | flops | bytes accessed | tf_op | source)
XLA Modules:
  0.0 118.4 jit_solution(17672093253367623393)
XLA Ops:
  0.6 77.2 %gather.1 = (f32[512,2048]{1,0:T(8,128)}, f32[1280,128]{1,0:T(8,128)}) custom-call(f32[256,1,4096]{2,1,0:T(1,128)} %x_ref.1), custom_call_target="tpu_custom_call" | custom-call | tf_op jit(solution)/shard_map/gather/pallas_call | solution.py:279
  77.8 37.3 %linear.1 = (f32[512,512]{1,0:T(8,128)}, f32[512,128]{1,0:T(8,128)}, f32[128,2048]{1,0:T(8,128)}) custom-call(f32[1280,128]{1,0:T(8,128)} %get-tuple-element.8.packed_ref, f32[512,128]{1,0:T(8,128)} %start_ref.1, f32[512,2048]{1,0:T(8,128)} %get-tuple-element.9.flat_ref), custom_call_target="tpu_custom_call" | custom-call | tf_op jit(solution)/shard_map/linear/pallas_call | solution.py:353
  115.1 3.3 %copy.5 = f32[128,1,2048]{2,1,0:T(1,128)} copy(f32[128,1,2048]{2,0,1:T(8,128)} %bitcast.1) | data formatting | bytes 2097152

commit v3 on v2

--- a/solution.py
+++ b/solution.py
@@ -108,17 +108,46 @@
     return stages
 
 
-def gather_kernel(modes, cols, x_ref, flat_ref, total_ref, acc, main, cross, *rest):
+def round_up(value, unit):
+    return -(-value // unit) * unit
+
+
+def layout_of(size, modes, cols):
+    pairs = lower_blocks(size // BLOCK)
+    rows = size // modes
+    inner = []
+    if rows % BLOCK == 0 and modes > 1:
+        inner = lower_blocks(rows // BLOCK)
+    per = rows // BLOCK
+    extent = round_up(len(inner) * BLOCK, 8 * cols)
+    where = {}
+    for m in range(modes):
+        for n, (i, k) in enumerate(inner):
+            where[m * per + i, m * per + k] = m * extent + n * BLOCK
+    outer = [pair for pair in pairs if pair not in where]
+    for n, pair in enumerate(outer):
+        where[pair] = modes * extent + n * BLOCK
+    return where, inner, extent, outer, round_up(len(outer) * BLOCK, 8 * modes * cols)
+
+
+def members_of(stages, modes):
+    return [count * (modes if with_mode else 1) for _, count, with_mode in stages]
+
+
+def gather_kernel(modes, cols, x_ref, flat_ref, total_ref, local, acc_in, acc_out, main, cross, *rest):
     mode, col = lax.axis_index("mode"), lax.axis_index("col")
-    stages = stages_of(modes, cols)
-    slots = rest[: len(stages)]
-    own_sem, piece_send, piece_recv, sum_send, sum_recv, share_send, share_recv = rest[len(stages) :]
+    all_stages = stages_of(modes, cols)
+    col_stages = [(stride, count, False) for stride, count, _ in all_stages]
+    n = len(all_stages)
+    slots_in, slots_out = rest[:n], rest[n : 2 * n]
+    local_sem, piece_send, piece_recv, swap_send, swap_recv, in_sems, out_sems, share_in, share_out = rest[2 * n :]
     rows, depth, length = x_ref.shape
     size = rows * modes
     width = length // modes
     chunk = min(CHUNK, width)
     per = width // chunk
     chunks = depth * per
+    where, inner, in_extent, outer, out_extent = layout_of(size, modes, cols)
 
     def position(stage):
         stride, count, with_mode = stage
@@ -136,14 +165,16 @@
         return other, (lax.rem(other, modes) if with_mode else mode, there)
 
     partners = [(lax.rem(mode + d, modes), col) for d in range(1, modes)]
-    greeted = [] if any(stage[2] for stage in stages) else list(partners)
-    for stage in stages:
+    greeted = []
+    for stage in all_stages:
         greeted += [peer(stage, d)[1] for d in range(1, members(stage))]
     barrier = pltpu.get_barrier_semaphore()
     for device in greeted:
         pl.semaphore_signal(barrier, inc=1, device_id=device, device_id_type=MESH)
     pl.semaphore_wait(barrier, len(greeted))
 
+    own_rows = pl.ds(pl.multiple_of(mode * rows, rows), rows)
+
     def spans(c):
         layer, part = lax.div(c, per), lax.rem(c, per)
         return layer, part * chunk, pl.multiple_of(layer * width + part * chunk, chunk)
@@ -151,105 +182,159 @@
     def piece(c, d):
         layer, start, target = spans(c)
         source = pl.multiple_of(lax.rem(mode + d, modes) * width + start, chunk)
-        place = pl.ds(pl.multiple_of(mode * rows, rows), rows)
         return pltpu.make_async_remote_copy(
             src_ref=x_ref.at[:, layer, pl.ds(source, chunk)],
-            dst_ref=flat_ref.at[place, pl.ds(target, chunk)],
+            dst_ref=flat_ref.at[own_rows, pl.ds(target, chunk)],
             send_sem=piece_send.at[d - 1, c],
             recv_sem=piece_recv.at[d - 1, c],
             device_id=partners[d - 1],
             device_id_type=MESH,
         )
 
-    def own(c):
-        layer, start, target = spans(c)
-        source = pl.multiple_of(mode * width + start, chunk)
-        place = pl.ds(pl.multiple_of(mode * rows, rows), rows)
+    def load(c):
+        layer, part = lax.div(c, per * modes), lax.rem(c, per * modes)
+        source = pl.multiple_of(part * chunk, chunk)
+        target = pl.multiple_of(layer * length + part * chunk, chunk)
         return pltpu.make_async_copy(
-            x_ref.at[:, layer, pl.ds(source, chunk)], flat_ref.at[place, pl.ds(target, chunk)], own_sem.at[c]
-        )
+            x_ref.at[:, layer, pl.ds(source, chunk)], local.at[:, pl.ds(target, chunk)], local_sem.at[c]
+        ), target
 
     def begin(c, carry):
         for d in range(1, modes):
             piece(c, d).start()
-        own(c).start()
         return carry
 
-    lax.fori_loop(0, chunks, begin, 0)
+    def begin_load(c, carry):
+        load(c)[0].start()
+        return carry
+
+    early = max(chunks // 2, 1)
+    lax.fori_loop(0, early, begin, 0)
+    lax.fori_loop(0, chunks * modes, begin_load, 0)
+
     main[...] = jnp.zeros_like(main)
     cross[...] = jnp.zeros_like(cross)
 
-    def accumulate(c, carry):
-        own(c).wait()
+    def accumulate_in(c, carry):
+        copy, target = load(c)
+        copy.wait()
+        if inner:
+            high, low = halves(local[:, pl.ds(target, chunk)])
+            main[0:rows, 0:rows] += contract(high, high, NT)
+            cross[0:rows, 0:rows] += contract(high, low, NT)
+        return carry
+
+    lax.fori_loop(0, chunks * modes, accumulate_in, 0)
+    for layer in range(depth):
+        source = pl.multiple_of(layer * length + mode * width, chunk)
+        flat_ref[own_rows, layer * width : (layer + 1) * width] = local[:, pl.ds(source, width)]
+
+    def pack(acc, pairs, extent):
+        for at, (i, k) in enumerate(pairs):
+            tall, wide = slice(i * BLOCK, (i + 1) * BLOCK), slice(k * BLOCK, (k + 1) * BLOCK)
+            acc[at * BLOCK : (at + 1) * BLOCK, :] = main[tall, wide] + (cross[tall, wide] + cross[wide, tall].T)
+        used = len(pairs) * BLOCK
+        if used < extent:
+            acc[used:, :] = jnp.zeros((extent - used, BLOCK), jnp.float32)
+
+    def scatter_sum(stages, acc, extent, slots, sems, target):
+        base, bases = 0, []
+        for g, stage in enumerate(stages):
+            count = members(stage)
+            part = extent // count
+            copies = []
+            for d in range(1, count):
+                other, device = peer(stage, d)
+                copy = pltpu.make_async_remote_copy(
+                    src_ref=acc.at[pl.ds(pl.multiple_of(base + other * part, 8), part), :],
+                    dst_ref=slots[g].at[d - 1],
+                    send_sem=sems.at[0, g, d - 1],
+                    recv_sem=sems.at[1, g, d - 1],
+                    device_id=device,
+                    device_id_type=MESH,
+                )
+                copy.start()
+                copies.append(copy)
+            base = base + position(stage) * part
+            extent = part
+            bases.append((base, part))
+            for copy in copies:
+                copy.wait()
+            mine = pl.ds(pl.multiple_of(base, 8), part)
+            added = acc[mine, :]
+            for d in range(1, count):
+                added = added + slots[g][d - 1]
+            if g < len(stages) - 1:
+                acc[mine, :] = added
+            else:
+                total_ref[pl.ds(pl.multiple_of(target + base, 8), part), :] = added
+        return bases
+
+    def share(stages, bases, targets, sems):
+        for g in reversed(range(len(stages))):
+            stage = stages[g]
+            base, part = bases[g]
+            copies = []
+            for d in range(1, members(stage)):
+                for t, target in enumerate(targets):
+                    mine = pl.ds(pl.multiple_of(target + base, 8), part)
+                    copy = pltpu.make_async_remote_copy(
+                        src_ref=total_ref.at[mine, :],
+                        dst_ref=total_ref.at[mine, :],
+                        send_sem=sems.at[0, g, (d - 1) * len(targets) + t],
+                        recv_sem=sems.at[1, g, (d - 1) * len(targets) + t],
+                        device_id=peer(stage, d)[1],
+                        device_id_type=MESH,
+                    )
+                    copy.start()
+                    copies.append(copy)
+            for copy in copies:
+                copy.wait()
+
+    def accumulate_out(c, carry):
         for d in range(1, modes):
             piece(c, d).wait_recv()
-        target = spans(c)[2]
-        high, low = halves(flat_ref[:, pl.ds(target, chunk)])
-        main[...] += contract(high, high, NT)
-        cross[...] += contract(high, low, NT)
+        high, low = halves(flat_ref[:, pl.ds(spans(c)[2], chunk)])
+        if inner:
+            for m in range(1, modes):
+                tall, wide = slice(m * rows, (m + 1) * rows), slice(0, m * rows)
+                main[tall, wide] += contract(high[tall, :], high[wide, :], NT) + contract(low[tall, :], high[wide, :], NT)
+                cross[tall, wide] += contract(high[tall, :], low[wide, :], NT)
+        else:
+            main[...] += contract(high, high, NT)
+            cross[...] += contract(high, low, NT)
         return carry
 
-    lax.fori_loop(0, chunks, accumulate, 0)
-
-    blocks = size // BLOCK
-    pairs = lower_blocks(blocks)
-    for n, (i, k) in enumerate(pairs):
-        tall, wide = slice(i * BLOCK, (i + 1) * BLOCK), slice(k * BLOCK, (k + 1) * BLOCK)
-        acc[n * BLOCK : (n + 1) * BLOCK, :] = main[tall, wide] + (cross[tall, wide] + cross[wide, tall].T)
-    used = len(pairs) * BLOCK
-    if used < acc.shape[0]:
-        acc[used:, :] = jnp.zeros((acc.shape[0] - used, BLOCK), jnp.float32)
-
-    base, extent = 0, acc.shape[0]
-    bases = []
-    for g, stage in enumerate(stages):
-        count = members(stage)
-        part = extent // count
-        copies = []
-        for d in range(1, count):
-            other, device = peer(stage, d)
-            copy = pltpu.make_async_remote_copy(
-                src_ref=acc.at[pl.ds(pl.multiple_of(base + other * part, 8), part), :],
-                dst_ref=slots[g].at[d - 1],
-                send_sem=sum_send.at[g, d - 1],
-                recv_sem=sum_recv.at[g, d - 1],
-                device_id=device,
+    swaps = []
+    if inner:
+        pack(acc_in, inner, in_extent)
+        main[...] = jnp.zeros_like(main)
+        cross[...] = jnp.zeros_like(cross)
+        bases = scatter_sum(col_stages, acc_in, in_extent, slots_in, in_sems, mode * in_extent)
+        base, part = bases[-1]
+        mine = pl.ds(pl.multiple_of(mode * in_extent + base, 8), part)
+        for d in range(1, modes):
+            swap = pltpu.make_async_remote_copy(
+                src_ref=total_ref.at[mine, :],
+                dst_ref=total_ref.at[mine, :],
+                send_sem=swap_send.at[d - 1],
+                recv_sem=swap_recv.at[d - 1],
+                device_id=partners[d - 1],
                 device_id_type=MESH,
             )
-            copy.start()
-            copies.append(copy)
-        base = base + position(stage) * part
-        extent = part
-        bases.append((base, part))
-        for copy in copies:
-            copy.wait()
-        mine = pl.ds(pl.multiple_of(base, 8), part)
-        added = acc[mine, :]
-        for d in range(1, count):
-            added = added + slots[g][d - 1]
-        if g < len(stages) - 1:
-            acc[mine, :] = added
-        else:
-            total_ref[mine, :] = added
-
-    for g in reversed(range(len(stages))):
-        stage = stages[g]
-        base, part = bases[g]
-        mine = pl.ds(pl.multiple_of(base, 8), part)
-        copies = []
-        for d in range(1, members(stage)):
-            copy = pltpu.make_async_remote_copy(
-                src_ref=total_ref.at[mine, :],
-                dst_ref=total_ref.at[mine, :],
-                send_sem=share_send.at[g, d - 1],
-                recv_sem=share_recv.at[g, d - 1],
-                device_id=peer(stage, d)[1],
-                device_id_type=MESH,
-            )
-            copy.start()
-            copies.append(copy)
-        for copy in copies:
-            copy.wait()
+            swap.start()
+            swaps.append(swap)
+    lax.fori_loop(early, chunks, begin, 0)
+    lax.fori_loop(0, early, accumulate_out, 0)
+    if inner:
+        for swap in swaps:
+            swap.wait()
+        share(col_stages, bases, [m * in_extent for m in range(modes)], share_in)
+    lax.fori_loop(early, chunks, accumulate_out, 0)
+
+    pack(acc_out, outer, out_extent)
+    bases = scatter_sum(all_stages, acc_out, out_extent, slots_out, out_sems, modes * in_extent)
+    share(all_stages, bases, [modes * in_extent], share_out)
 
     def end(c, carry):
         for d in range(1, modes):
@@ -266,16 +351,19 @@
     width = length // modes
     chunks = depth * (width // min(CHUNK, width))
     stages = stages_of(modes, cols)
-    unit = 8 * modes * cols
-    packed = -(-(len(lower_blocks(size // BLOCK)) * BLOCK) // unit) * unit
-    slots, extent, most = [], packed, 1
+    _, inner, in_extent, _, out_extent = layout_of(size, modes, cols)
+    in_extent = max(in_extent, 8 * cols)
+    slots_in, slots_out, extent_in, extent, most = [], [], in_extent, out_extent, 1
     for stride, count, with_mode in stages:
+        extent_in = extent_in // count
+        slots_in.append(pltpu.VMEM((max(count - 1, 1), extent_in, BLOCK), jnp.float32))
         count = count * (modes if with_mode else 1)
         extent = extent // count
+        slots_out.append(pltpu.VMEM((max(count - 1, 1), extent, BLOCK), jnp.float32))
         most = max(most, count - 1)
-        slots.append(pltpu.VMEM((max(count - 1, 1), extent, BLOCK), jnp.float32))
     dma = pltpu.SemaphoreType.DMA
     vmem = pl.BlockSpec(memory_space=pltpu.VMEM)
+    packed = (modes * in_extent if inner else 0) + out_extent
     return pl.pallas_call(
         functools.partial(gather_kernel, modes, cols),
         out_shape=(
@@ -285,28 +373,33 @@
         in_specs=[pl.BlockSpec(memory_space=pl.ANY)],
         out_specs=(vmem, vmem),
         scratch_shapes=[
-            pltpu.VMEM((packed, BLOCK), jnp.float32),
+            pltpu.VMEM((rows, depth * length), jnp.float32),
+            pltpu.VMEM((in_extent, BLOCK), jnp.float32),
+            pltpu.VMEM((out_extent, BLOCK), jnp.float32),
             pltpu.VMEM((size, size), jnp.float32),
             pltpu.VMEM((size, size), jnp.float32),
-            *slots,
-            dma((chunks,)),
-            dma((max(modes - 1, 1), chunks)),
-            dma((max(modes - 1, 1), chunks)),
-            *[dma((len(stages), most))] * 4,
+            *slots_in,
+            *slots_out,
+            dma((chunks * modes,)),
+            *[dma((max(modes - 1, 1), chunks))] * 2,
+            *[dma((max(modes - 1, 1),))] * 2,
+            *[dma((2, len(stages), most))] * 2,
+            dma((2, len(stages), most * modes)),
+            dma((2, len(stages), most)),
         ],
         compiler_params=pltpu.CompilerParams(collective_id=0, has_side_effects=True),
         name="gather",
     )(tensor)
 
 
-def linear_kernel(columns, packed_ref, start_ref, flat_ref, factor_ref, basis_ref, core_ref, gram, work, image, aug_f, aug_b):
+def linear_kernel(columns, where, packed_ref, start_ref, flat_ref, factor_ref, basis_ref, core_ref, gram, work, image, aug_f, aug_b, core, core_sem):
     size, rank = start_ref.shape
     blocks = size // BLOCK
     row = lax.broadcasted_iota(jnp.int32, (BLOCK, BLOCK), 0)
     column = lax.broadcasted_iota(jnp.int32, (BLOCK, BLOCK), 1)
     scale = 1.0 / columns
-    for n, (i, k) in enumerate(lower_blocks(blocks)):
-        scaled = packed_ref[n * BLOCK : (n + 1) * BLOCK, :] * scale
+    for (i, k), at in where.items():
+        scaled = packed_ref[at : at + BLOCK, :] * scale
         gram[i * BLOCK : (i + 1) * BLOCK, k * BLOCK : (k + 1) * BLOCK] = scaled
         work[i * BLOCK : (i + 1) * BLOCK, k * BLOCK : (k + 1) * BLOCK] = scaled
         if i != k:
@@ -339,32 +432,45 @@
                 work[below:size, below:size] = work[below:size, below:size] - exact(left, left, NT)
 
     high, low = halves(basis_ref[...])
-    width = 512
-    for start in range(0, flat_ref.shape[1], width):
-        flat_high, flat_low = halves(flat_ref[:, start : start + width])
-        core_ref[:, start : start + width] = (
-            contract(high, flat_high, TN) + contract(high, flat_low, TN) + contract(low, flat_high, TN)
+    depth, length = core_ref.shape[1:]
+    width = min(CHUNK, length)
+    copies = []
+    for start in range(0, depth * length, width):
+        part = slice(start, start + width)
+        flat_high, flat_low = halves(flat_ref[:, part])
+        core[:, part] = contract(high, flat_high, TN) + contract(high, flat_low, TN) + contract(low, flat_high, TN)
+        layer, offset = divmod(start, length)
+        copy = pltpu.make_async_copy(
+            core.at[:, part], core_ref.at[:, layer, offset : offset + width], core_sem.at[len(copies)]
         )
-
-
-def linear(columns, packed, start_basis, flat):
+        copy.start()
+        copies.append(copy)
+    for copy in copies:
+        copy.wait()
+
+
+def linear(columns, depth, packed, start_basis, flat):
     size, rank = start_basis.shape
+    length = flat.shape[1] // depth
+    where = layout_of(size, lax.axis_size("mode"), lax.axis_size("col"))[0]
     vmem = pl.BlockSpec(memory_space=pltpu.VMEM)
     return pl.pallas_call(
-        functools.partial(linear_kernel, columns),
+        functools.partial(linear_kernel, columns, where),
         out_shape=(
             jax.ShapeDtypeStruct((size, size), jnp.float32),
             jax.ShapeDtypeStruct((size, rank), jnp.float32),
-            jax.ShapeDtypeStruct((rank, flat.shape[1]), jnp.float32),
+            jax.ShapeDtypeStruct((rank, depth, length), jnp.float32),
         ),
         in_specs=[vmem] * 3,
-        out_specs=(vmem,) * 3,
+        out_specs=(vmem, vmem, pl.BlockSpec(memory_space=pl.ANY)),
         scratch_shapes=[
             pltpu.VMEM((size, size), jnp.float32),
             pltpu.VMEM((size, size), jnp.float32),
             pltpu.VMEM((size, rank), jnp.float32),
             pltpu.VMEM((BLOCK, 2 * BLOCK), jnp.float32),
             pltpu.VMEM((rank, 2 * rank), jnp.float32),
+            pltpu.VMEM((rank, flat.shape[1]), jnp.float32),
+            pltpu.SemaphoreType.DMA((flat.shape[1] // min(CHUNK, length),)),
         ],
         name="linear",
     )(packed, start_basis, flat)
@@ -374,8 +480,8 @@
     depth = tensor.shape[1]
     flat, packed = gather(tensor)
     columns = flat.shape[1] * lax.axis_size("mode") * lax.axis_size("col")
-    factor, basis, core = linear(columns, packed, start_basis, flat)
-    return (factor, basis, core.reshape(basis.shape[1], depth, -1))
+    factor, basis, core = linear(columns, depth, packed, start_basis, flat)
+    return (factor, basis, core)
 
 
 def solution(mesh):

time: 119 us -> 113 us (0.950)
  local copies, waits for them, and re-layouts: 3.27 us -> 0 us
  Pallas kernels: 114 us -> 112 us
    pallas_call x1, Pallas kernels: 77.2 us -> 73.3 us  [gather(): pl.pallas_call(functools.partial(gather_kernel, modes, cols), out_shape=(...]
    unnamed x1 -> x0, local copies, waits for them, and re-layouts: 3.27 us -> none
    pallas_call x1, Pallas kernels: 37.3 us -> 38.5 us  [linear(): pl.pallas_call(functools.partial(linear_kernel, columns, where), out_shap...]
where the time goes in v3:
time: 113 us
  Pallas kernels  112 us (99%)
    pallas_call x1, Pallas kernels, gather(): pl.pallas_call(functools.partial(gather_kernel, modes, cols), out_shape=(...  73.3 us
    pallas_call x1, Pallas kernels, linear(): pl.pallas_call(functools.partial(linear_kernel, columns, where), out_shap...  38.5 us

profile of v3, /device:TPU:0, one launch (start us, length us, event | category | flops | bytes accessed | tf_op | source)
XLA Modules:
  0.0 112.6 jit_solution(11883949148700334848)
XLA Ops:
  0.6 73.3 %gather.1 = (f32[512,2048]{1,0:T(8,128)}, f32[1280,128]{1,0:T(8,128)}) custom-call(f32[256,1,4096]{2,1,0:T(1,128)} %x_ref.1), custom_call_target="tpu_custom_call" | custom-call | tf_op jit(solution)/shard_map/gather/pallas_call | solution.py:367
  73.9 38.5 %linear.1 = (f32[512,512]{1,0:T(8,128)}, f32[512,128]{1,0:T(8,128)}, f32[128,1,2048]{2,1,0:T(1,128)}) custom-call(f32[1280,128]{1,0:T(8,128)} %get-tuple-element.5.packed_ref, f32[512,128]{1,0:T(8,128)} %start_ref.1, f32[512,2048]{1,0:T(8,128)} %get-tuple-element.6.flat_ref), custom_call_target="tpu_custom_call" | custom-call | tf_op jit(solution)/shard_map/linear/pallas_call | solution.py:457
